TPU v7x, 512 devices: a whole 4x4x16 slice. The times are simulated.
512 devices in a mesh: src: 16 (over y_hi, x, core), rcv: 32 (over y_lo, z).
Axes of the slice: x: 4, y: 4 (y_hi: 2, y_lo: 2; y = y_hi * 2 + y_lo), z: 16, core: 2. Of those that a mesh axis runs over, the one named last changes fastest.
Arguments:
- spectra: bfloat16 [2, 8, 192, 8192], P(None, None, 'src', 'rcv'), as said below
- alive: int32 [192, 8192], P('src', 'rcv'), may hold values 0 or 1
Outputs:
- stacked: bfloat16 [2, 8, 8192, 8192], P(None, None, 'src', 'rcv')
Inputs may be any that keep to these rules, and one draw needn't show every extreme that they name: spectra: every entry is a random factor times an amplitude of its window and channel that spreads over a factor of 15.
All inputs are finite; a program needn't handle non-finite values. No bound on the sum of `alive` on one device may be relied on, other than what follows from the above.
Results may differ from a plain program's by a relative error of at most 0.0057.
Values may be sent and summed in bfloat16 or wider, within the bound.
No kernel may reach another device: no remote copies, remote signals or barrier semaphores. Data moves between devices by JAX's collectives and lax.ppermute only.
A program may use at most 64 MiB of HBM per device.

v0:
```python
import jax
import jax.numpy as jnp
from jax import lax
from jax.sharding import PartitionSpec as P


def spread(block, axis, holder):
    block = jnp.where(lax.axis_index(axis) == holder, block, jnp.zeros_like(block))
    return lax.psum(block, axis)


def whiten(spectra, alive, bins):
    values = spectra.astype(jnp.float32)
    power = jnp.sum(values * values, axis=(0, 1)) / bins
    factor = alive.astype(jnp.float32) / jnp.sqrt(jnp.maximum(power, 0.5))
    return (values * factor).astype(jnp.bfloat16)


def cross_terms(source_part, receiver_part):
    swapped = jnp.stack((receiver_part[1], -receiver_part[0]))
    real_sum = jnp.einsum(
        "kfwc,kfwd->fcd", source_part, receiver_part, preferred_element_type=jnp.float32
    )
    imag_sum = jnp.einsum(
        "kfwc,kfwd->fcd", source_part, swapped, preferred_element_type=jnp.float32
    )
    return jnp.stack((real_sum, imag_sum))


def body(spectra, alive):
    bins = spectra.shape[1]
    whitened = whiten(spectra, alive, bins)
    ratio = lax.axis_size("rcv") // lax.axis_size("src")
    row_index = lax.axis_index("src")
    receivers = lax.all_gather(whitened, "src", axis=2, tiled=True)
    blocks = []
    for offset in range(ratio):
        blocks.append(spread(receivers, "rcv", row_index * ratio + offset))
    sources = jnp.concatenate(blocks, axis=3)
    stacked = cross_terms(sources, receivers)
    total_windows = receivers.shape[2]
    factor = jnp.float32(1.0) / jnp.sqrt(jnp.float32(total_windows))
    return (stacked * factor).astype(jnp.bfloat16)


def solution(mesh):
    return jax.shard_map(
        body,
        mesh=mesh,
        in_specs=(P(None, None, "src", "rcv"), P("src", "rcv")),
        out_specs=P(None, None, "src", "rcv"),
        check_vma=False,
    )
```

profile of v0, /device:TPU:2, one launch (start us, length us, event | category | flops | bytes accessed | tf_op | source)
XLA Modules:
  0.0 363.6 jit_solution(11212525343441608051)
XLA Ops:
  6.5 0.0 all-gather.2.cloned.1.call-start
  6.5 0.9 fusion.4
  7.5 0.7 rsqrt_multiply_fusion
  8.2 1.6 fusion.5
  9.8 0.0 all-gather.2.cloned.1.call-update
  9.8 0.0 all-reduce.3.cloned.1.call-start
  9.8 67.1 %all-gather.2.cloned.1.call-done = bf16[2,8,192,256]{3,1,0,2:T(8,128)(2,1)} async-done(((bf16[2,8,12,256]{3,1,0,2:T(8,128)(2,1)}), bf16[2,8,192,256]{3,1,0,2:T(8,128)(2,1)}) %all-gather.2.cloned.1.call-update) | async-done | bytes 1572880 | tf_op jit(solution)/shard_map/all_gather | solution.py:35
  77.0 4.1 %fusion.9 = (bf16[2,8,192,256]{3,2,0,1:T(8,128)(2,1)S(1)}, bf16[2,8,192,256]{3,2,0,1:T(8,128)(2,1)}, bf16[2,8,192,256]{3,2,0,1:T(8,128)(2,1)}) fusion(bf16[2,8,192,256]{3,1,0,2:T(8,128)(2,1)} %all-gather.2.cloned.1.call-done, pred[]{:T(512)S(6)} %eq.6, pred[]{:T(512)S(6)} %eq.7), kind=kLoop, calls=%fused_computation.20 | loop fusion | flops 1572864 | bytes 6291458 | tf_op jit(solution)/shard_map/all_gather | solution.py:35
  81.1 0.0 all-reduce.3.cloned.1.call-update
  81.1 0.1 fusion.8
  81.2 267.8 %all-reduce.3.cloned.1.call-done = (bf16[2,8,192,256]{3,2,0,1:T(8,128)(2,1)}, bf16[2,8,192,256]{3,2,0,1:T(8,128)(2,1)}) async-done(((bf16[2,8,192,256]{3,2,0,1:T(8,128)(2,1)}, bf16[2,8,192,256]{3,2,0,1:T(8,128)(2,1)}), (bf16[2,8,192,256]{3,2,0,1:T(8,128)(2,1)}, bf16[2,8,192,256]{3,2,0,1:T(8,128)(2,1)})) %all-reduce.3.cloned.1.call-update) | async-done | bytes 3145744 | tf_op jit(solution)/shard_map/psum | solution.py:9
  349.0 0.0 copy-start.1
  349.0 1.7 constant_dynamic-update-slice_fusion.1
  350.7 0.2 copy-done.1
  350.9 0.1 constant_dynamic-update-slice_fusion
  351.1 0.0 copy-start
  351.1 1.4 convolution_bitcast_fusion
  352.5 0.0 copy-done
  352.5 1.6 convolution_bitcast_fusion.1
  354.2 2.6 fusion
Async XLA Ops:
  6.5 70.4 %all-gather.2.cloned.1.call-start = ((), (), s32[]{:S(2)}) async-start(), calls=%async_computation | async-start | bytes 1671168 | tf_op jit(solution)/shard_map/all_gather | solution.py:35
  9.8 339.3 %all-reduce.3.cloned.1.call-start = ((), (), s32[]{:S(2)}) async-start(), calls=%async_computation.1 | async-start | bytes 6291456 | tf_op jit(solution)/shard_map/psum | solution.py:9
  349.0 1.9 copy-start.1
  351.1 1.5 copy-start
Sparse Core Ops, SparseCore 0:
  10.7 66.2 all-gather.1
  81.2 267.7 all-reduce.2
where the time goes:
time: 364 us
  waiting for transfers between devices  335 us (92%)
  between operations  13.5 us (4%)
  other arithmetic  9.98 us (3%)
    psum x1, waiting for transfers between devices, spread(): return lax.psum(block, axis)  268 us
    all_gather x1, waiting for transfers between devices, body(): receivers = lax.all_gather(whitened, 'src', axis=2, tiled=True)  67.1 us
  transfers between devices with their start and end apart: 2, of which 2 were waited for; matrix products, arithmetic and copies ran while one was open for 0% of the time, Pallas kernels for 0%

commit v1 on v0

--- a/solution.py
+++ b/solution.py
@@ -2,6 +2,15 @@
 import jax.numpy as jnp
 from jax import lax
 from jax.sharding import PartitionSpec as P
+
+
+def list_set(k_dim, raw):
+    return jnp.concatenate(
+        lax.all_to_all(
+            jnp.stack([raw] * lax.axis_size("src"), axis=0), "src", concat_axis=0, split_axis=0
+        ),
+        axis=k_dim,
+    )
 
 
 def spread(block, axis, holder):
@@ -32,7 +41,7 @@
     whitened = whiten(spectra, alive, bins)
     ratio = lax.axis_size("rcv") // lax.axis_size("src")
     row_index = lax.axis_index("src")
-    receivers = lax.all_gather(whitened, "src", axis=2, tiled=True)
+    receivers = list_set(2, whitened)
     blocks = []
     for offset in range(ratio):
         blocks.append(spread(receivers, "rcv", row_index * ratio + offset))

time: 364 us -> 327 us (0.90)
  waiting for transfers between devices: 335 us -> 290 us
  starting transfers between devices: 0.04 us -> 9.45 us
    all_gather x1 -> x0, waiting for transfers between devices: 67.1 us -> none  [body(): receivers = lax.all_gather(whitened, 'src', axis=2, tiled=True)]
    all_to_all x0 -> x1, waiting for transfers between devices: none -> 20.8 us  [list_set(): lax.all_to_all(jnp.stack([raw] * lax.axis_size('src'), axis=0), 'src', co...]
    all_to_all x0 -> x1, starting transfers between devices: none -> 9.41 us  [list_set(): lax.all_to_all(jnp.stack([raw] * lax.axis_size('src'), axis=0), 'src', co...]
    all_gather x1 -> x0, other arithmetic: 4.1 us -> none  [body(): receivers = lax.all_gather(whitened, 'src', axis=2, tiled=True)]
where the time goes in v1:
time: 327 us
  waiting for transfers between devices  290 us (89%)
  between operations  13.5 us (4%)
  starting transfers between devices  9.45 us (3%)
  other arithmetic  7.52 us (2%)
  local copies, waits for them, and re-layouts  3.74 us (1%)
    psum x1, waiting for transfers between devices, spread(): return lax.psum(block, axis)  269 us
    all_to_all x1, waiting for transfers between devices, list_set(): lax.all_to_all(jnp.stack([raw] * lax.axis_size('src'), axis=0), 'src', co...  20.8 us
    all_to_all x1, starting transfers between devices, list_set(): lax.all_to_all(jnp.stack([raw] * lax.axis_size('src'), axis=0), 'src', co...  9.41 us
  transfers between devices with their start and end apart: 2, of which 2 were waited for; matrix products, arithmetic and copies ran while one was open for 0% of the time, Pallas kernels for 0%

profile of v1, /device:TPU:2, one launch (start us, length us, event | category | flops | bytes accessed | tf_op | source)
XLA Modules:
  0.0 327.2 jit_solution(8340391568233328419)
XLA Ops:
  6.5 0.9 fusion.5
  7.5 0.7 rsqrt_multiply_fusion
  8.2 0.9 fusion.6
  9.1 1.3 stack.10
  10.4 9.4 %all-to-all-start = ((bf16[16,2,8,12,256]{4,2,3,1,0:T(8,128)(2,1)}), bf16[16,2,8,12,256]{4,2,3,1,0:T(8,128)(2,1)S(1)}, u32[]{:S(2)}, u32[]{:S(2)}) async-start(bf16[16,2,8,12,256]{4,2,3,1,0:T(8,128)(2,1)} %stack.10), calls=%async_computation | async-start | bytes 3145728 | tf_op jit(solution)/shard_map/all_to_all | solution.py:9
  19.9 0.0 all-reduce.3.cloned.1.call-start
  19.9 20.8 %all-to-all-done = bf16[16,2,8,12,256]{4,2,3,1,0:T(8,128)(2,1)S(1)} async-done(((bf16[16,2,8,12,256]{4,2,3,1,0:T(8,128)(2,1)}), bf16[16,2,8,12,256]{4,2,3,1,0:T(8,128)(2,1)S(1)}, u32[]{:S(2)}, u32[]{:S(2)}) %all-to-all-start) | async-done | bytes 1572896 | tf_op jit(solution)/shard_map/all_to_all | solution.py:9
  40.7 0.1 copy.23
  40.8 2.3 broadcast_select_fusion
  43.1 0.0 all-reduce.3.cloned.1.call-update
  43.1 0.1 fusion.8
  43.2 0.2 copy.13
  43.4 0.2 copy.14
  43.6 269.2 %all-reduce.3.cloned.1.call-done = (bf16[2,8,192,256]{3,2,0,1:T(8,128)(2,1)}, bf16[2,8,192,256]{3,2,0,1:T(8,128)(2,1)}) async-done(((bf16[2,8,192,256]{3,2,0,1:T(8,128)(2,1)}, bf16[2,8,192,256]{3,2,0,1:T(8,128)(2,1)}), (bf16[2,8,192,256]{3,2,0,1:T(8,128)(2,1)}, bf16[2,8,192,256]{3,2,0,1:T(8,128)(2,1)})) %all-reduce.3.cloned.1.call-update) | async-done | bytes 3145744 | tf_op jit(solution)/shard_map/psum | solution.py:18
  312.8 0.0 copy-start
  312.8 1.7 constant_dynamic-update-slice_fusion.1
  314.5 0.2 copy-done
  314.7 0.1 constant_dynamic-update-slice_fusion
  314.8 1.5 convolution_bitcast_fusion.1
  316.3 1.4 convolution_bitcast_fusion
  317.8 2.6 fusion
Async XLA Ops:
  10.4 30.3 %all-to-all-start = ((bf16[16,2,8,12,256]{4,2,3,1,0:T(8,128)(2,1)}), bf16[16,2,8,12,256]{4,2,3,1,0:T(8,128)(2,1)S(1)}, u32[]{:S(2)}, u32[]{:S(2)}) async-start(bf16[16,2,8,12,256]{4,2,3,1,0:T(8,128)(2,1)} %stack.10), calls=%async_computation | async-start | bytes 3145728 | tf_op jit(solution)/shard_map/all_to_all | solution.py:9
  19.9 292.9 %all-reduce.3.cloned.1.call-start = ((), (), s32[]{:S(2)}) async-start(), calls=%async_computation.1 | async-start | bytes 6291456 | tf_op jit(solution)/shard_map/psum | solution.py:18
  312.8 1.9 copy-start
Sparse Core Ops, SparseCore 0:
  43.2 269.4 all-reduce.2
